TPU v7x, 32 devices: a whole 2x2x4 slice. The times are simulated.
32 devices in a mesh: col: 4 (over y, x), tile: 8 (over z, core).
Axes of the slice: x: 2, y: 2, z: 4, core: 2. Of those that a mesh axis runs over, the one named last changes fastest.
Arguments:
- acquired: float32 [8192, 2, 1, 4096], P('tile', None, None, 'col'), may hold values from -6 to 6
- flatfield: float32 [2, 1024], replicated, may hold values from 0.5 to 1.5
- tile_gain: float32 [8, 4, 2], P('tile', 'col'), may hold values from 0.5 to 2
- subvoxel: float32 [8, 4, 2], P('tile', 'col'), may hold values from 0 to 1
- band_offset: int32 [8, 4, 2], P('tile', 'col'), may hold values from -2 to 2
- row_owner: int32 [8, 4, 1024, 1], P('tile', 'col'), may hold values from 0 to 31; in each aligned block of 1024 rows (0 to 1023, 1024 to 2047, ..., all dimensions but the last counted through in order) at most 48 rows name the same one
Outputs:
- owned_rows: float32 [49152, 2, 1, 1024], P(('col', 'tile'))
Inputs may be any that keep to these rules, and one draw needn't show every extreme that they name: `row_owner`: no tile names one owner for more than 48 of its rows; some tile names some owner exactly 48 times.
All inputs are finite; a program needn't handle non-finite values.
Results may differ from a plain program's by a relative error of at most 0.0003.
Values sent between devices are 32-bit elements; how exact they have to be, the bound alone decides.
No kernel may reach another device: no remote copies, remote signals or barrier semaphores. Data moves between devices by JAX's collectives and lax.ppermute only.
A program may use at most 192 MiB of HBM per device.

v0:
```python
import math

import jax
import jax.numpy as jnp
from jax import lax
from jax.sharding import PartitionSpec as P

MARGIN = 128


def with_halo(cells, sides, width):
    for axis, dim in sides:
        count = lax.axis_size(axis)
        ends = count - 1
        head = lax.slice_in_dim(cells, 0, width, axis=dim)
        tail = lax.slice_in_dim(cells, cells.shape[dim] - width, cells.shape[dim], axis=dim)
        cells = jnp.concatenate(
            [
                lax.ppermute(tail, axis, [(i, (i + 1) % count) for i in range(ends)]),
                cells,
                lax.ppermute(head, axis, [((i + 1) % count, i) for i in range(ends)]),
            ],
            axis=dim,
        )
    return cells


def cubic_matrix(fraction, offset, length):
    cube = fraction * fraction * fraction
    square = fraction * fraction
    weights = (
        -0.5 * cube + square - 0.5 * fraction,
        1.5 * cube - 2.5 * square + 1.0,
        -1.5 * cube + 2.0 * square + 0.5 * fraction,
        0.5 * cube - 0.5 * square,
    )
    target = jnp.arange(length, dtype=jnp.int32)[:, None]
    source = jnp.arange(length, dtype=jnp.int32)[None, :]
    matrix = jnp.zeros((length, length), jnp.float32)
    for place, weight in zip((-1, 0, 1, 2), weights):
        picked = jnp.clip(target + offset + place, 0, length - 1)
        matrix = matrix + jnp.where(source == picked, weight, jnp.float32(0.0))
    return matrix


def blend_ramps(length, has_prev, has_next):
    place = jnp.arange(length).astype(jnp.float32)
    rising = jnp.square(jnp.sin(0.5 * math.pi * (place + 0.5) / MARGIN))
    falling = jnp.square(jnp.cos(0.5 * math.pi * (place - (length - MARGIN) + 0.5) / MARGIN))
    head = place < MARGIN
    tail = place >= length - MARGIN
    before = jnp.where(head, has_prev * (1.0 - rising), 0.0)
    own = jnp.where(
        head,
        has_prev * rising + 1.0 - has_prev,
        jnp.where(tail, has_next * falling + 1.0 - has_next, 1.0),
    )
    after = jnp.where(tail, has_next * (1.0 - falling), 0.0)
    return jnp.stack([before, own, after])


def shards(acquired, flatfield, tile_gain, subvoxel, band_offset, row_owner):
    height, channels, planes, columns = acquired.shape
    corrected = acquired * flatfield[None, :, None, :] * tile_gain[0, 0][None, :, None, None]
    row_matrix = cubic_matrix(subvoxel[0, 0, 0], band_offset[0, 0, 0], height)
    col_matrix = cubic_matrix(subvoxel[0, 0, 1], band_offset[0, 0, 1], columns)
    along_rows = jnp.dot(
        row_matrix,
        corrected.reshape(height, channels * planes * columns),
        precision=lax.Precision.HIGHEST,
        preferred_element_type=jnp.float32,
    )
    resampled = jnp.dot(
        along_rows.reshape(height * channels * planes, columns),
        col_matrix.T,
        precision=lax.Precision.HIGHEST,
        preferred_element_type=jnp.float32,
    )
    resampled = resampled.reshape(height, channels, planes, columns)
    extended = with_halo(resampled, (("col", 3), ("tile", 0)), MARGIN)
    tile_place = lax.axis_index("tile")
    col_place = lax.axis_index("col")
    row_weights = blend_ramps(
        height,
        (tile_place > 0).astype(jnp.float32),
        (tile_place < lax.axis_size("tile") - 1).astype(jnp.float32),
    )
    col_weights = blend_ramps(
        columns,
        (col_place > 0).astype(jnp.float32),
        (col_place < lax.axis_size("col") - 1).astype(jnp.float32),
    )
    joined = jnp.zeros(resampled.shape, jnp.float32)
    for above in range(3):
        for beside in range(3):
            window = extended[
                above * MARGIN : above * MARGIN + height,
                :,
                :,
                beside * MARGIN : beside * MARGIN + columns,
            ]
            joined = (
                joined
                + row_weights[above][:, None, None, None]
                * col_weights[beside][None, None, None, :]
                * window
            )
    devices = lax.axis_size("col") * lax.axis_size("tile")
    slots = max(2, (3 * height + 2 * devices - 1) // (2 * devices))
    owner = row_owner[0, 0, :, 0]
    onehot = (owner[:, None] == jnp.arange(devices, dtype=jnp.int32)[None, :]).astype(jnp.int32)
    earlier = jnp.cumsum(onehot, axis=0) - onehot
    rank = jnp.sum(earlier * onehot, axis=1)
    slot = owner * slots + rank
    outgoing = (
        jnp.zeros((devices * slots, channels, planes, columns), jnp.float32).at[slot].set(joined)
    )
    arrived = lax.all_to_all(outgoing, ("col", "tile"), split_axis=0, concat_axis=0, tiled=True)
    return arrived


def solution(mesh):
    placed = (
        P("tile", None, None, "col"),
        P(),
        P("tile", "col", None),
        P("tile", "col", None),
        P("tile", "col", None),
        P("tile", "col", None, None),
    )
    return jax.shard_map(
        shards,
        mesh=mesh,
        in_specs=placed,
        out_specs=P(("col", "tile"), None, None, None),
        check_vma=False,
    )
```

profile of v0, /device:TPU:0, one launch (start us, length us, event | category | flops | bytes accessed | tf_op | source)
XLA Modules:
  0.0 722.8 jit_solution(8919707603676714431)
XLA Ops:
  0.0 1.3 fusion.68
  3.6 1.3 fusion.67
  4.9 0.7 add_clamp_fusion.3
  5.6 0.7 add_clamp_fusion.5
  8.8 0.6 add_clamp_fusion
  9.4 0.6 add_clamp_fusion.2
  10.0 33.2 %multiply_reduce_fusion = f32[1024,2,1024]{2,1,0:T(2,128)S(1)} fusion(f32[1024,2,1,1024]{3,2,1,0:T(1,128)} %param.6, f32[2]{0:T(128)} %bitcast.47, f32[2,1024]{1,0:T(2,128)} %param.7), kind=kLoop, calls=%fused_computation.33 | loop fusion | flops 4194304 | bytes 16785416 | tf_op jit(solution)/shard_map/mul | solution.py:64
  43.2 7.5 %copy.10 = f32[128,8,2,1024]{3,1,2,0:T(8,128)} copy(f32[128,8,2,1024]{3,2,1,0:T(2,128)S(1)} %bitcast.39) | data formatting | bytes 16777216
  50.8 34.8 %fusion.29 = f32[1024,2048]{1,0:T(8,128)} fusion(f32[1024,2048]{1,0:T(8,128)} %bitcast.40, f32[]{:T(128)S(6)} %sub.87, s32[1024]{0:T(1024)S(1)} %get-tuple-element.22, f32[]{:T(128)S(6)} %add.288, s32[1024]{0:T(1024)S(1)} %get-tuple-element.23, f32[]{:T(128)S(6)} %add.284, s32[1024]{0:T(1024)S(1)} %get-tuple-element.25, f32[]{:T(128)S(6)} %sub.85, ...), kind=kOutput, calls=%fused_computation.47 | convolution fusion | flops 25781338112 | bytes 16793616 | tf_op jit(solution)/shard_map/dot_general | solution.py:67
  85.6 9.3 %reshape.446 = f32[2048,1024]{1,0:T(8,128)} reshape(f32[1024,2048]{1,0:T(8,128)} %fusion.29) | data formatting | bytes 16777216 | tf_op jit(solution)/shard_map/reshape | solution.py:74
  94.9 1.6 fusion.74
  96.5 30.6 %fusion.21 = f32[2048,1024]{1,0:T(8,128)} fusion(f32[2048,1024]{1,0:T(8,128)} %reshape.446, f32[1024,1024]{1,0:T(8,128)S(1)} %fusion.74), kind=kOutput, calls=%fused_computation.35 | convolution fusion | flops 25769803776 | bytes 20971520 | tf_op jit(solution)/shard_map/dot_general | solution.py:73
  127.1 10.6 %reshape.447 = f32[1024,2,1,1024]{3,1,0,2:T(2,128)} reshape(f32[2048,1024]{1,0:T(8,128)} %fusion.21) | data formatting | bytes 16777216 | tf_op jit(solution)/shard_map/reshape | solution.py:79
  137.7 2.7 fusion.66
  140.4 4.9 collective-permute-start
  145.3 1.3 collective-permute-start.1
  146.6 0.0 copy-done.4
  146.6 9.3 %reduce-window.6 = s32[32,8,128]{2,1,0:T(8,128)S(1)} reduce-window(s32[32,8,128]{2,1,0:T(8,128)S(1)} %fusion.58, s32[]{:T(128)} %constant.25.clone.1), window={size=1x1x128 pad=0_0x0_0x127_0}, to_apply=%region_0.1 | reduce-window | flops 4161536 | bytes 262148 | tf_op jit(solution)/shard_map/reduce-window
  155.9 0.1 slice.80
  156.0 0.1 copy.7
  156.2 0.1 copy.8
  156.3 0.1 broadcast_add_fusion
  156.4 0.1 multiply_select_fusion
  156.5 11.5 %collective-permute-done = f32[1024,2,1,128]{3,1,0,2:T(2,128)S(1)} collective-permute-done((f32[1024,2,1,128]{3,1,0,2:T(2,128)}, f32[1024,2,1,128]{3,1,0,2:T(2,128)S(1)}, u32[]{:S(2)}, u32[]{:S(2)}) %collective-permute-start) | collective-permute-done | bytes 1048608 | tf_op jit(solution)/shard_map/ppermute | solution.py:19
  167.9 0.4 constant_dynamic-update-slice_fusion.2
  168.3 4.7 constant_dynamic-update-slice_fusion.1
  173.0 0.0 copy-done.2
  173.0 19.3 %collective-permute-done.1 = f32[1024,2,1,128]{3,1,0,2:T(2,128)S(1)} collective-permute-done((f32[1024,2,1,128]{3,1,0,2:T(2,128)S(1)}, f32[1024,2,1,128]{3,1,0,2:T(2,128)S(1)}, u32[]{:S(2)}, u32[]{:S(2)}) %collective-permute-start.1) | collective-permute-done | bytes 1048608 | tf_op jit(solution)/shard_map/ppermute | solution.py:21
  192.3 0.4 constant_dynamic-update-slice_fusion
  192.7 0.0 copy-start
  192.7 4.1 copy-done
  196.8 2.5 fusion.65
  199.2 2.4 collective-permute-start.2
  201.6 1.3 collective-permute-start.3
  202.9 0.1 select_select_fusion.1
  203.0 0.1 select_select_fusion
  203.0 0.0 copy-done.3
  203.0 0.0 copy-start.1
  203.0 14.9 %broadcast_multiply_fusion.8 = (f32[1024,1024]{1,0:T(8,128)}, f32[1024,1024]{1,0:T(8,128)}, f32[1024,1024]{1,0:T(8,128)}, f32[1024,1024]{1,0:T(8,128)}, f32[1024...) fusion(f32[1024]{0:T(1024)S(1)} %get-tuple-element.31, ...), kind=kLoop, calls=%fused_computation.85 | loop fusion | flops 9437184 | bytes 37773312 | tf_op jit(solution)/shard_map/mul | solution.py:104
  218.0 0.0 collective-permute-done.2
  218.0 0.0 collective-permute-done.3
  218.0 0.0 copy-done.1
  218.0 84.3 %fusion.20 = f32[1024,2,1024]{2,1,0:T(2,128)} fusion(f32[128,2,1,1280]{3,1,0,2:T(2,128)} %collective-permute-done.3, f32[1024,2,1,1280]{3,1,0,2:T(2,128)S(1)} %copy-done.1, f32[1024,2,1,128]{3,1,0,2:T(2,128)} %copy-done.3, f32[1024,2,1,1024]{3,1,0,2:T(2,128)} %reshape.447, f32[1024,2,1,128]{3,1,0,2:T(2,128)} %copy-done.2, ...), kind=kLoop, calls=%fused_computation.34 | loop fusion | flops 52428800 | bytes 69730304 | tf_op jit(solution)/shard_map/add | solution.py:103
  302.3 4.8 broadcast.589
  307.2 118.1 %scatter_fusion = f32[1536,2,1024]{2,1,0:T(2,128)} fusion(f32[1536,2,1024]{2,1,0:T(2,128)} %broadcast.589, s32[1024]{0:T(1024)S(1)} %bitcast.46, f32[1024,2,1024]{2,1,0:T(2,128)} %fusion.20), kind=kCustom, calls=%fused_computation | custom fusion | bytes 25169920 | tf_op jit(solution)/shard_map/scatter | solution.py:116
  425.3 10.3 %reshape.451 = f32[1536,2,1,1024]{3,2,1,0:T(1,128)S(1)} reshape(f32[1536,2,1024]{2,1,0:T(2,128)} %scatter_fusion) | data formatting | bytes 25165824 | tf_op jit(solution)/shard_map/scatter | solution.py:116
  435.5 282.0 %all_to_all.5 = f32[1536,2,1,1024]{3,2,1,0:T(1,128)S(1)} all-to-all(f32[1536,2,1,1024]{3,2,1,0:T(1,128)S(1)} %reshape.451), channel_id=1, replica_groups=mesh['col'=4,'tile'=8] {'col','tile'}, dimensions={0} | all-to-all | bytes 25165824 | tf_op jit(solution)/shard_map/all_to_all | solution.py:118
  717.6 4.8 copy.16
  (8 shorter events, 0.1 us)
Async XLA Ops:
  127.1 19.5 %copy-start.4 = (s32[1,1,1024,1]{2,3,1,0:T(1,128)S(1)}, s32[1,1,1024,1]{2,3,1,0:T(1,128)}, u32[]{:S(2)}) copy-start(s32[1,1,1024,1]{2,3,1,0:T(1,128)} %param.11) | copy-start | bytes 12292
  140.4 27.6 %collective-permute-start = (f32[1024,2,1,128]{3,1,0,2:T(2,128)}, f32[1024,2,1,128]{3,1,0,2:T(2,128)S(1)}, u32[]{:S(2)}, u32[]{:S(2)}) collective-permute-start(f32[1024,2,1,128]{3,1,0,2:T(2,128)} %get-tuple-element.8), channel_id=1, source_target_pairs={{0,8},{8,16},{16,24},{1,9},{9,17},{17,25},{2,10},{10,18},{18,26},{... | collective-permute-start | bytes 3145736 | tf_op jit(solution)/shard_map/ppermute | solution.py:19
  145.3 47.0 %collective-permute-start.1 = (f32[1024,2,1,128]{3,1,0,2:T(2,128)S(1)}, f32[1024,2,1,128]{3,1,0,2:T(2,128)S(1)}, u32[]{:S(2)}, u32[]{:S(2)}) collective-permute-start(f32[1024,2,1,128]{3,1,0,2:T(2,128)S(1)} %get-tuple-element.7), channel_id=1, source_target_pairs={{8,0},{16,8},{24,16},{9,1},{17,9},{25,17},{10,2},{18,10},{26,18},{... | collective-permute-start | bytes 3145736 | tf_op jit(solution)/shard_map/ppermute | solution.py:21
  167.9 5.0 copy-start.2
  192.3 10.8 %copy-start.3 = (f32[1024,2,1,128]{3,1,0,2:T(2,128)}, f32[1024,2,1,128]{3,1,0,2:T(2,128)S(1)}, u32[]{:S(2)}) copy-start(f32[1024,2,1,128]{3,1,0,2:T(2,128)S(1)} %collective-permute-done.1) | copy-start | bytes 3145732
  192.7 4.1 copy-start
  199.2 18.7 %collective-permute-start.2 = (f32[128,2,1,1280]{3,1,0,2:T(2,128)}, f32[128,2,1,1280]{3,1,0,2:T(2,128)}, u32[]{:S(2)}, u32[]{:S(2)}) collective-permute-start(f32[128,2,1,1280]{3,1,0,2:T(2,128)} %get-tuple-element.5), channel_id=1, source_target_pairs={{0,1},{1,2},{2,3},{3,4},{4,5},{5,6},{6,7},{8,9},{9,10},{10,11},{11... | collective-permute-start | bytes 3932168 | tf_op jit(solution)/shard_map/ppermute | solution.py:19
  201.6 16.4 %collective-permute-start.3 = (f32[128,2,1,1280]{3,1,0,2:T(2,128)}, f32[128,2,1,1280]{3,1,0,2:T(2,128)}, u32[]{:S(2)}, u32[]{:S(2)}) collective-permute-start(f32[128,2,1,1280]{3,1,0,2:T(2,128)} %get-tuple-element.6), channel_id=1, source_target_pairs={{1,0},{2,1},{3,2},{4,3},{5,4},{6,5},{7,6},{9,8},{10,9},{11,10},{12... | collective-permute-start | bytes 3932168 | tf_op jit(solution)/shard_map/ppermute | solution.py:21
  203.0 14.9 %copy-start.1 = (f32[1024,2,1,1280]{3,1,0,2:T(2,128)S(1)}, f32[1024,2,1,1280]{3,1,0,2:T(2,128)}, u32[]{:S(2)}) copy-start(f32[1024,2,1,1280]{3,1,0,2:T(2,128)} %copy-done) | copy-start | bytes 31457284
where the time goes:
time: 733 us; the launch traced here: 723 us
  blocking collectives  282 us (38%)
  local copies, waits for them, and re-layouts  183 us (25%)
  other arithmetic  146 us (20%)
  matrix products  65.4 us (9%)
  waiting for transfers between devices  30.7 us (4%)
  starting transfers between devices  9.86 us (1%)
    all_to_all x1, blocking collectives, shards(): lax.all_to_all(outgoing, ('col', 'tile'), split_axis=0, concat_axis=0, ti...  282 us
    scatter x2, local copies, waits for them, and re-layouts, shards(): jnp.zeros((devices * slots, channels, planes, columns), jnp.float32)  128 us
    add x1, other arithmetic, shards(): joined + row_weights[above][:, None, None, None] * col_weights[beside][No...  84.3 us
    dot_general x1, matrix products, shards(): jnp.dot(row_matrix, corrected.reshape(height, channels * planes * columns...  34.8 us
    mul x1, other arithmetic, shards(): acquired * flatfield[None, :, None, :]  33.2 us
    dot_general x1, matrix products, shards(): jnp.dot(along_rows.reshape(height * channels * planes, columns), col_matr...  30.6 us
    unnamed x14, local copies, waits for them, and re-layouts  21.4 us
    ppermute x2, waiting for transfers between devices, with_halo(): lax.ppermute(head, axis, [((i + 1) % count, i) for i in range(ends)])  19.3 us
  transfers between devices with their start and end apart: 4, of which 2 were waited for; matrix products, arithmetic and copies ran while one was open for 4% of the time, Pallas kernels for 0%

commit v1 on v0

v1 whole, which is shorter than its diff:
```python
import math

import jax
import jax.numpy as jnp
from jax import lax
from jax.experimental import pallas as pl
from jax.experimental.pallas import tpu as pltpu
from jax.sharding import PartitionSpec as P

MARGIN = 128
LANES = 128
TAPS = (-1, 0, 1, 2)


def cubic_weights(f):
    square = f * f
    cube = square * f
    return (
        -0.5 * cube + square - 0.5 * f,
        1.5 * cube - 2.5 * square + 1.0,
        -1.5 * cube + 2.0 * square + 0.5 * f,
        0.5 * cube - 0.5 * square,
    )


def resample_rows(sub, off, gain, owner, x, field, out, head, tail, left, right, source, count, *,
                  height, step_rows, window, slots, devices, planes):
    step = pl.program_id(0)
    per = out.shape[0] // step_rows
    blocks = out.shape[1]
    start = jnp.clip(step * step_rows - 4, 0, height - window)
    row_w = cubic_weights(sub[0])
    col_w = cubic_weights(sub[1])
    row_off = off[0]
    col_off = off[1]
    edge_steps = MARGIN // step_rows
    steps = height // step_rows

    @pl.when(step == 0)
    def _():
        @pl.loop(0, devices * slots)
        def _(s):
            source[s] = height

        @pl.loop(0, devices)
        def _(d):
            count[d] = 0

    lane = lax.broadcasted_iota(jnp.int32, (per, blocks, LANES), 2)
    block = lax.broadcasted_iota(jnp.int32, (per, blocks, LANES), 1)
    first_block = block == 0
    last_block = block == blocks - 1
    takes_up = [lane < col_off + k for k in TAPS]
    takes_down = [lane >= LANES + col_off + k for k in TAPS]
    turns = [(LANES - col_off - k) & (LANES - 1) for k in TAPS]
    scale = jnp.stack([field[c // planes] * gain[c // planes] for c in range(per)])

    @pl.loop(0, step_rows, unroll=8)
    def _(r):
        row = step * step_rows + r
        y = None
        for k, w in zip(TAPS, row_w):
            at = jnp.clip(row + row_off + k, 0, height - 1) - start
            part = x[pl.ds(at * per, per)] * w
            y = part if y is None else y + part
        y = y * scale
        up = jnp.where(last_block, y[:, blocks - 1 :, LANES - 1 :], pltpu.roll(y, blocks - 1, 1))
        down = jnp.where(first_block, y[:, :1, :1], pltpu.roll(y, 1, 1))
        z = None
        for k in range(4):
            mixed = jnp.where(takes_up[k], up, jnp.where(takes_down[k], down, y))
            part = pltpu.roll(mixed, turns[k], 2) * col_w[k]
            z = part if z is None else z + part
        out[pl.ds(r * per, per)] = z
        left[pl.ds(r * per, per), :] = z[:, 0, :]
        right[pl.ds(r * per, per), :] = z[:, blocks - 1, :]
        d = owner[row]
        rank = count[d]
        count[d] = rank + 1
        source[d * slots + rank] = row

    @pl.when(step < edge_steps)
    def _():
        head[...] = out[...]

    @pl.when(step >= steps - edge_steps)
    def _():
        tail[...] = out[...]


def blend_and_place(source, row_w, col_w, own, left, right, above, below, corner_al, corner_ar,
                    corner_bl, corner_br, out, joined, *, height, per):
    step = pl.program_id(0)

    @pl.when(step == 0)
    def _():
        before = col_w[0]
        mine = col_w[1]
        after = col_w[2]

        def across(mid, lo, hi, i):
            lo_v = jnp.broadcast_to(lo[pl.ds(i, 1), :], mine.shape)
            hi_v = jnp.broadcast_to(hi[pl.ds(i, 1), :], mine.shape)
            return mine * mid[i] + before * lo_v + after * hi_v

        @pl.loop(0, MARGIN * per, unroll=8)
        def _(i):
            r = i // per
            joined[i] = row_w[1, r] * across(own, left, right, i) + row_w[0, r] * across(
                above, corner_al, corner_ar, i)

        @pl.loop(MARGIN * per, (height - MARGIN) * per, unroll=8)
        def _(i):
            joined[i] = across(own, left, right, i)

        @pl.loop(0, MARGIN * per, unroll=8)
        def _(t):
            i = t + (height - MARGIN) * per
            r = i // per
            joined[i] = row_w[1, r] * across(own, left, right, i) + row_w[2, r] * across(
                below, corner_bl, corner_br, t)

        joined[height * per : (height + 1) * per] = jnp.zeros((per,) + joined.shape[1:], jnp.float32)

    here = out.shape[0] // per

    @pl.loop(0, here, unroll=8)
    def _(s):
        r = source[step * here + s]
        out[pl.ds(s * per, per)] = joined[pl.ds(r * per, per)]


def blend_ramps(length, has_prev, has_next):
    place = jnp.arange(length).astype(jnp.float32)
    rising = jnp.square(jnp.sin(0.5 * math.pi * (place + 0.5) / MARGIN))
    falling = jnp.square(jnp.cos(0.5 * math.pi * (place - (length - MARGIN) + 0.5) / MARGIN))
    head = place < MARGIN
    tail = place >= length - MARGIN
    before = jnp.where(head, has_prev * (1.0 - rising), 0.0)
    own = jnp.where(
        head,
        has_prev * rising + 1.0 - has_prev,
        jnp.where(tail, has_next * falling + 1.0 - has_next, 1.0),
    )
    after = jnp.where(tail, has_next * (1.0 - falling), 0.0)
    return jnp.stack([before, own, after])


def shards(acquired, flatfield, tile_gain, subvoxel, band_offset, row_owner):
    height, channels, planes, columns = acquired.shape
    per = channels * planes
    blocks = columns // LANES
    cols, tiles = lax.axis_size("col"), lax.axis_size("tile")
    devices = cols * tiles
    slots = max(2, (3 * height + 2 * devices - 1) // (2 * devices))
    f32 = jnp.float32
    smem = pl.BlockSpec(memory_space=pltpu.SMEM)

    step_rows = math.gcd(64, height)
    steps = height // step_rows
    window = step_rows + 8
    edge_steps = MARGIN // step_rows
    edge = MARGIN * per
    row_block = (step_rows * per, blocks, LANES)

    def window_start(i):
        return (jnp.clip(i * step_rows - 4, 0, height - window) * per, 0, 0)

    resampled, head, tail, left, right, source = pl.pallas_call(
        lambda *refs: resample_rows(*refs, height=height, step_rows=step_rows, window=window,
                                    slots=slots, devices=devices, planes=planes),
        grid=(steps,),
        in_specs=[
            smem, smem, smem, smem,
            pl.BlockSpec((pl.Element(window * per), pl.Element(blocks), pl.Element(LANES)), window_start),
            pl.BlockSpec((channels, blocks, LANES), lambda i: (0, 0, 0)),
        ],
        out_specs=[
            pl.BlockSpec(row_block, lambda i: (i, 0, 0)),
            pl.BlockSpec(row_block, lambda i: (jnp.minimum(i, edge_steps - 1), 0, 0)),
            pl.BlockSpec(row_block, lambda i: (jnp.maximum(i - (steps - edge_steps), 0), 0, 0)),
            pl.BlockSpec((step_rows * per, LANES), lambda i: (i, 0)),
            pl.BlockSpec((step_rows * per, LANES), lambda i: (i, 0)),
            smem,
        ],
        out_shape=[
            jax.ShapeDtypeStruct((height * per, blocks, LANES), f32),
            jax.ShapeDtypeStruct((edge, blocks, LANES), f32),
            jax.ShapeDtypeStruct((edge, blocks, LANES), f32),
            jax.ShapeDtypeStruct((height * per, LANES), f32),
            jax.ShapeDtypeStruct((height * per, LANES), f32),
            jax.ShapeDtypeStruct((devices * slots,), jnp.int32),
        ],
        scratch_shapes=[pltpu.SMEM((devices,), jnp.int32)],
        name="resample_rows",
    )(
        subvoxel.reshape(2),
        band_offset.reshape(2),
        tile_gain.reshape(channels),
        row_owner.reshape(height),
        acquired.reshape(height * per, blocks, LANES),
        flatfield.reshape(channels, blocks, LANES),
    )

    def shifted(value, dc, dt):
        pairs = []
        for c in range(cols):
            for t in range(tiles):
                if 0 <= c + dc < cols and 0 <= t + dt < tiles:
                    pairs.append((c * tiles + t, (c + dc) * tiles + t + dt))
        return lax.ppermute(value, ("col", "tile"), pairs)

    from_left = shifted(right, 1, 0)
    from_right = shifted(left, -1, 0)
    from_above = shifted(tail, 0, 1)
    from_below = shifted(head, 0, -1)
    corner_al = shifted(right[-edge:], 1, 1)
    corner_ar = shifted(left[-edge:], -1, 1)
    corner_bl = shifted(right[:edge], 1, -1)
    corner_br = shifted(left[:edge], -1, -1)

    tile_place = lax.axis_index("tile")
    col_place = lax.axis_index("col")
    row_weights = blend_ramps(height, (tile_place > 0).astype(f32), (tile_place < tiles - 1).astype(f32))
    col_weights = blend_ramps(columns, (col_place > 0).astype(f32), (col_place < cols - 1).astype(f32))

    group = math.gcd(devices, max(1, 96 // slots))
    whole3 = lambda n: pl.BlockSpec((n, blocks, LANES), lambda i: (0, 0, 0))
    whole2 = lambda n: pl.BlockSpec((n, LANES), lambda i: (0, 0))
    outgoing = pl.pallas_call(
        lambda *refs: blend_and_place(*refs, height=height, per=per),
        grid=(devices // group,),
        in_specs=[
            smem, smem, whole3(3), whole3(height * per), whole2(height * per), whole2(height * per),
            whole3(edge), whole3(edge), whole2(edge), whole2(edge), whole2(edge), whole2(edge),
        ],
        out_specs=pl.BlockSpec((group * slots * per, blocks, LANES), lambda i: (i, 0, 0)),
        out_shape=jax.ShapeDtypeStruct((devices * slots * per, blocks, LANES), f32),
        scratch_shapes=[pltpu.VMEM(((height + 1) * per, blocks, LANES), f32)],
        name="blend_and_place",
    )(
        source, row_weights, col_weights.reshape(3, blocks, LANES), resampled, from_left, from_right,
        from_above, from_below, corner_al, corner_ar, corner_bl, corner_br,
    )
    arrived = lax.all_to_all(outgoing, ("col", "tile"), split_axis=0, concat_axis=0, tiled=True)
    return arrived.reshape(devices * slots, channels, planes, columns)


def solution(mesh):
    placed = (
        P("tile", None, None, "col"),
        P(),
        P("tile", "col", None),
        P("tile", "col", None),
        P("tile", "col", None),
        P("tile", "col", None, None),
    )
    return jax.shard_map(
        shards,
        mesh=mesh,
        in_specs=placed,
        out_specs=P(("col", "tile"), None, None, None),
        check_vma=False,
    )
```

time: 733 us -> 445 us (0.61); the launches traced: 723 us -> 444 us
  local copies, waits for them, and re-layouts: 183 us -> 10.5 us
  other arithmetic: 146 us -> 1.73 us
  Pallas kernels: 0 us -> 74.2 us
  matrix products: 65.4 us -> 0 us
  starting transfers between devices: 9.86 us -> 59.3 us
  waiting for transfers between devices: 30.7 us -> 10.6 us
    scatter x2 -> x0, local copies, waits for them, and re-layouts: 128 us -> none  [shards(): jnp.zeros((devices * slots, channels, planes, columns), jnp.float32)]
    add x1 -> x0, other arithmetic: 84.3 us -> none  [shards(): joined + row_weights[above][:, None, None, None] * col_weights[beside][No...]
    pallas_call x0 -> x2, Pallas kernels: none -> 74.2 us  [the longest x1 54.7 us: shards(): pl.pallas_call(lambda *refs: resample_rows(*refs, height=height, step_row...]
    dot_general x2 -> x0, matrix products: 65.4 us -> none  [the longest x1 34.8 us: shards(): jnp.dot(row_matrix, corrected.reshape(height, channels * planes * columns...]
    ppermute x4 -> x8, starting transfers between devices: 9.86 us -> 59.3 us  [shifted(): return lax.ppermute(value, ('col', 'tile'), pairs)]
    mul x2 -> x0, other arithmetic: 48.2 us -> none  [the longest x1 33.2 us: shards(): acquired * flatfield[None, :, None, :]]
    ppermute x4 -> x8, waiting for transfers between devices: 30.7 us -> 10.6 us  [shifted(): return lax.ppermute(value, ('col', 'tile'), pairs)]
    reshape x2 -> x0, local copies, waits for them, and re-layouts: 19.9 us -> none  [the longest x1 10.6 us: shards(): resampled = resampled.reshape(height, channels, planes, columns)]
  transfers between devices with their start and end apart: 4 -> 8, of which waited for: 2 -> 2; matrix products, arithmetic and copies ran while one was open for 4% -> 1% of each run, Pallas kernels for 0% -> 0%
where the time goes in v1:
time: 445 us; the launch traced here: 444 us
  blocking collectives  288 us (65%)
  Pallas kernels  74.2 us (17%)
  starting transfers between devices  59.3 us (13%)
  waiting for transfers between devices  10.6 us (2%)
  local copies, waits for them, and re-layouts  10.5 us (2%)
    all_to_all x1, blocking collectives, shards(): lax.all_to_all(outgoing, ('col', 'tile'), split_axis=0, concat_axis=0, ti...  288 us
    ppermute x8, starting transfers between devices, shifted(): return lax.ppermute(value, ('col', 'tile'), pairs)  59.3 us
    pallas_call x1, Pallas kernels, shards(): pl.pallas_call(lambda *refs: resample_rows(*refs, height=height, step_row...  54.7 us
    pallas_call x1, Pallas kernels, shards(): pl.pallas_call(lambda *refs: blend_and_place(*refs, height=height, per=pe...  19.5 us
    ppermute x8, waiting for transfers between devices, shifted(): return lax.ppermute(value, ('col', 'tile'), pairs)  10.6 us
  transfers between devices with their start and end apart: 8, of which 2 were waited for; matrix products, arithmetic and copies ran while one was open for 1% of the time, Pallas kernels for 0%

profile of v1, /device:TPU:0, one launch (start us, length us, event | category | flops | bytes accessed | tf_op | source)
XLA Modules:
  0.0 444.3 jit_solution(17934567873778464336)
XLA Ops:
  0.0 1.3 copy.10
  1.3 54.7 %resample_rows.1 = (f32[2048,8,128]{2,1,0:T(8,128)}, f32[256,8,128]{2,1,0:T(8,128)}, f32[256,8,128]{2,1,0:T(8,128)}, f32[2048,128]{1,0:T(8,128)}, f32[2048,128]{1,0:T(8,128)}, /*index=5*/s32[1536]{0:T(1024)}) custom-call(f32[2]{0:T(128)} %bitcast.15, s32[2]{0:T(128)} %bitcast.16, f32[2]{0:T(128)} %bitcast.17, s32[1024]{0:T(1024)} %bitcast.14, ...), custom_call_target="tpu_custom_call" | custom-call | tf_op jit(solution)/shard_map/resample_rows/pallas_call | solution.py:169
  56.0 2.5 collective-permute-start.2
  58.5 1.3 collective-permute-start.3
  59.8 4.3 collective-permute-start
  64.0 1.3 collective-permute-start.1
  65.3 1.0 fusion.1
  66.3 0.7 collective-permute-start.6
  67.0 1.7 fusion
  68.7 0.0 collective-permute-done.6.refs_10_
  68.7 0.0 copy-start.3
  68.7 47.4 %collective-permute-start.4 = (f32[256,128]{1,0:T(8,128)S(1)}, f32[256,128]{1,0:T(8,128)S(1)}, u32[]{:S(2)}, u32[]{:S(2)}) collective-permute-start(f32[256,128]{1,0:T(8,128)S(1)} %get-tuple-element.20), channel_id=1, source_target_pairs={{0,9},{1,10},{2,11},{3,12},{4,13},{5,14},{6,15},{8,17},{9,18},{10,... | collective-permute-start | bytes 393224 | tf_op jit(solution)/shard_map/ppermute | solution.py:211
  116.1 0.1 multiply_select_fusion
  116.2 0.3 compare_select_fusion
  116.4 2.2 collective-permute-done.4.refs_8_
  118.6 0.0 copy-start.4
  118.6 1.3 collective-permute-start.7
  119.9 0.1 multiply_select_fusion.1
  120.0 0.6 pad_maximum_fusion.1.refs_2_
  120.6 8.5 %collective-permute-done.7.refs_11_ = f32[256,128]{1,0:T(8,128)S(1)} collective-permute-done((f32[256,128]{1,0:T(8,128)}, f32[256,128]{1,0:T(8,128)S(1)}, u32[]{:S(2)}, u32[]{:S(2)}) %collective-permute-start.7) | collective-permute-done | bytes 131104 | tf_op jit(solution)/shard_map/ppermute | solution.py:211
  129.0 0.0 copy-start.5
  129.0 0.7 collective-permute-start.5
  129.7 0.1 compare_select_fusion.3
  129.8 0.6 pad_maximum_fusion.refs_1_
  130.5 0.0 collective-permute-done.5.refs_9_
  130.5 0.0 copy-start.6
  130.5 0.0 collective-permute-done.2.refs_6_
  130.5 0.0 copy-start
  130.5 0.0 collective-permute-done.3.refs_7_
  130.5 0.0 copy-start.1
  130.5 0.0 collective-permute-done.refs_4_
  130.5 0.6 copy-done.6
  131.1 0.0 copy-start.2
  131.1 0.0 collective-permute-done.1.refs_5_
  131.1 0.0 copy-done.3
  131.1 0.0 copy-done.4
  131.1 0.0 copy-done.5
  131.1 0.4 copy-done
  131.5 0.4 copy-done.1
  132.0 0.3 copy-done.2
  132.3 19.5 %blend_and_place.1 = f32[3072,8,128]{2,1,0:T(8,128)} custom-call(s32[1536]{0:T(1024)} %get-tuple-element.11.refs_0_, f32[3,1024]{1,0:T(4,128)} %pad_maximum_fusion.refs_1_, f32[3,8,128]{2,1,0:T(8,128)} %pad_maximum_fusion.1.refs_2_, f32[2048,8,128]{2,1,0:T(8,128)} %get-tuple-element.12.refs_3_, f32[2048,128]{1,0:T(8,128)} %copy-done.2, ...), custom_call_target="tpu_custom_call" | custom-call | tf_op jit(solution)/shard_map/blend_and_place/pallas_call | solution.py:230
  151.8 287.7 %all_to_all.5 = f32[3072,8,128]{2,1,0:T(8,128)S(1)} all-to-all(f32[3072,8,128]{2,1,0:T(8,128)} %blend_and_place.1), channel_id=1, replica_groups=mesh['col'=4,'tile'=8] {'col','tile'}, dimensions={0} | all-to-all | bytes 25165824 | tf_op jit(solution)/shard_map/all_to_all | solution.py:245
  439.5 4.8 %copy.12 = f32[1536,2,1,1024]{3,2,1,0:T(1,128)} copy(f32[1536,2,1,1024]{3,2,1,0:T(1,128)S(1)} %bitcast.10) | data formatting | bytes 25165824
Async XLA Ops:
  56.0 74.5 %collective-permute-start.2 = (f32[256,8,128]{2,1,0:T(8,128)}, f32[256,8,128]{2,1,0:T(8,128)S(1)}, u32[]{:S(2)}, u32[]{:S(2)}) collective-permute-start(f32[256,8,128]{2,1,0:T(8,128)} %get-tuple-element.15), channel_id=1, source_target_pairs={{0,1},{1,2},{2,3},{3,4},{4,5},{5,6},{6,7},{8,9},{9,10},{10,11},{11... | collective-permute-start | bytes 3145736 | tf_op jit(solution)/shard_map/ppermute | solution.py:211
  58.5 72.0 %collective-permute-start.3 = (f32[256,8,128]{2,1,0:T(8,128)}, f32[256,8,128]{2,1,0:T(8,128)S(1)}, u32[]{:S(2)}, u32[]{:S(2)}) collective-permute-start(f32[256,8,128]{2,1,0:T(8,128)} %get-tuple-element.16), channel_id=1, source_target_pairs={{1,0},{2,1},{3,2},{4,3},{5,4},{6,5},{7,6},{9,8},{10,9},{11,10},{12... | collective-permute-start | bytes 3145736 | tf_op jit(solution)/shard_map/ppermute | solution.py:211
  59.8 70.7 %collective-permute-start = (f32[2048,128]{1,0:T(8,128)}, f32[2048,128]{1,0:T(8,128)S(1)}, u32[]{:S(2)}, u32[]{:S(2)}) collective-permute-start(f32[2048,128]{1,0:T(8,128)} %get-tuple-element.13), channel_id=1, source_target_pairs={{0,8},{1,9},{2,10},{3,11},{4,12},{5,13},{6,14},{7,15},{8,16},{9,17... | collective-permute-start | bytes 3145736 | tf_op jit(solution)/shard_map/ppermute | solution.py:211
  64.0 67.1 %collective-permute-start.1 = (f32[2048,128]{1,0:T(8,128)}, f32[2048,128]{1,0:T(8,128)}, u32[]{:S(2)}, u32[]{:S(2)}) collective-permute-start(f32[2048,128]{1,0:T(8,128)} %get-tuple-element.14), channel_id=1, source_target_pairs={{8,0},{9,1},{10,2},{11,3},{12,4},{13,5},{14,6},{15,7},{16,8},{17,9... | collective-permute-start | bytes 3145736 | tf_op jit(solution)/shard_map/ppermute | solution.py:211
  66.3 2.4 collective-permute-start.6
  68.7 62.4 %copy-start.3 = (f32[256,128]{1,0:T(8,128)}, f32[256,128]{1,0:T(8,128)S(1)}, u32[]{:S(2)}) copy-start(f32[256,128]{1,0:T(8,128)S(1)} %collective-permute-done.6.refs_10_) | copy-start | bytes 393220
  68.7 49.9 %collective-permute-start.4 = (f32[256,128]{1,0:T(8,128)S(1)}, f32[256,128]{1,0:T(8,128)S(1)}, u32[]{:S(2)}, u32[]{:S(2)}) collective-permute-start(f32[256,128]{1,0:T(8,128)S(1)} %get-tuple-element.20), channel_id=1, source_target_pairs={{0,9},{1,10},{2,11},{3,12},{4,13},{5,14},{6,15},{8,17},{9,18},{10,... | collective-permute-start | bytes 393224 | tf_op jit(solution)/shard_map/ppermute | solution.py:211
  118.6 12.5 %copy-start.4 = (f32[256,128]{1,0:T(8,128)}, f32[256,128]{1,0:T(8,128)S(1)}, u32[]{:S(2)}) copy-start(f32[256,128]{1,0:T(8,128)S(1)} %collective-permute-done.4.refs_8_) | copy-start | bytes 393220
  118.6 10.4 %collective-permute-start.7 = (f32[256,128]{1,0:T(8,128)}, f32[256,128]{1,0:T(8,128)S(1)}, u32[]{:S(2)}, u32[]{:S(2)}) collective-permute-start(f32[256,128]{1,0:T(8,128)} %get-tuple-element.17), channel_id=1, source_target_pairs={{9,0},{10,1},{11,2},{12,3},{13,4},{14,5},{15,6},{17,8},{18,9},{19,... | collective-permute-start | bytes 393224 | tf_op jit(solution)/shard_map/ppermute | solution.py:211
  129.0 2.1 copy-start.5
  129.0 1.4 collective-permute-start.5
  130.5 0.7 copy-start.6
  130.5 1.1 copy-start
  130.5 1.5 copy-start.1
  131.1 1.2 copy-start.2
